TPU v7x, 32 devices: a whole 2x2x4 slice. The times are simulated.
32 devices in a mesh: groups: 2 (over y), tensor: 4 (over z), dp: 4 (over x, core).
Axes of the slice: x: 2, y: 2, z: 4, core: 2. Of those that a mesh axis runs over, the one named last changes fastest.
Arguments:
- tokens: bfloat16 [256, 8192], P(('groups', 'tensor', 'dp')), parts along dimension 0, may hold values from -6 to 6
- gate_projection_matrix: bfloat16 [8192, 14336], P('dp', 'tensor'), may hold values from -0.0625 to 0.0625
- up_projection_matrix: bfloat16 [8192, 14336], P('dp', 'tensor'), may hold values from -0.0625 to 0.0625
- down_projection_matrix: bfloat16 [14336, 8192], P('tensor', 'dp'), may hold values from -0.046875 to 0.046875
- gate_adapter_inmap: bfloat16 [16384, 64], P(('groups', 'dp')), parts along dimension 0, may hold values from -0.0625 to 0.0625
- gate_adapter_outmap: bfloat16 [64, 28672], P(None, ('groups', 'tensor')), parts along dimension 1, may hold values from -0.75 to 0.75
- up_adapter_inmap: bfloat16 [16384, 64], P(('groups', 'dp')), parts along dimension 0, may hold values from -0.0625 to 0.0625
- up_adapter_outmap: bfloat16 [64, 28672], P(None, ('groups', 'tensor')), parts along dimension 1, may hold values from -0.75 to 0.75
- down_adapter_inmap: bfloat16 [28672, 64], P(('groups', 'tensor')), parts along dimension 0, may hold values from -0.046875 to 0.046875
- down_adapter_outmap: bfloat16 [64, 16384], P(None, 'groups'), parts along dimension 1, may hold values from -0.75 to 0.75
Outputs:
- block_out: bfloat16 [256, 8192], P(('groups', 'tensor', 'dp')), parts along dimension 0
There are 2 independent parts, one for each index of `groups`. A program takes and returns all parts, laid end to end along the dimension named above; an argument that names none is the same for every part. Nothing has to cross between parts.
All inputs are finite; a program needn't handle non-finite values.
Results may differ from a plain program's by a relative error of at most 0.0053.
Values may be sent and summed in bfloat16 or wider, within the bound.
A program may use at most 256 MiB of HBM per device.

v0:
```python
import jax
import jax.numpy as jnp
from jax import lax
from jax.sharding import PartitionSpec as P

adapter_scale_factor = 0.5


def body(
    tokens,
    gate_projection_matrix,
    up_projection_matrix,
    down_projection_matrix,
    gate_adapter_inmap,
    gate_adapter_outmap,
    up_adapter_inmap,
    up_adapter_outmap,
    down_adapter_inmap,
    down_adapter_outmap,
):
    tok_dev = tokens.shape[0]
    n_tensor = lax.axis_size("tensor")
    n_dp = lax.axis_size("dp")
    hidden_unit_count = gate_projection_matrix.shape[1]
    adapter_rank_size = gate_adapter_inmap.shape[1]
    columns = lax.all_to_all(tokens, "dp", split_axis=1, concat_axis=0, tiled=True)
    stacked_lowrank = jnp.concatenate(
        [gate_projection_matrix, up_projection_matrix, gate_adapter_inmap, up_adapter_inmap], axis=1
    )
    partial_all = jnp.dot(
        lax.all_gather(columns, "tensor", axis=0, tiled=True),
        stacked_lowrank,
        preferred_element_type=jnp.float32,
    )
    partial_all = partial_all.reshape(n_tensor, n_dp, tok_dev, partial_all.shape[1])
    summed_lowrank = lax.psum_scatter(partial_all, "dp", scatter_dimension=1, tiled=True)
    summed_lowrank = summed_lowrank.reshape(n_tensor * tok_dev, summed_lowrank.shape[3])
    gate_dense_part = summed_lowrank[:, :hidden_unit_count]
    up_dense_part = summed_lowrank[:, hidden_unit_count : 2 * hidden_unit_count]
    gate_lowrank_part = summed_lowrank[
        :, 2 * hidden_unit_count : 2 * hidden_unit_count + adapter_rank_size
    ].astype(jnp.bfloat16)
    up_lowrank_part = summed_lowrank[:, 2 * hidden_unit_count + adapter_rank_size :].astype(
        jnp.bfloat16
    )
    gate_activated = gate_dense_part + adapter_scale_factor * jnp.dot(
        gate_lowrank_part, gate_adapter_outmap, preferred_element_type=jnp.float32
    )
    up_projected_value = up_dense_part + adapter_scale_factor * jnp.dot(
        up_lowrank_part, up_adapter_outmap, preferred_element_type=jnp.float32
    )
    hidden_product = (jax.nn.silu(gate_activated) * up_projected_value).astype(jnp.bfloat16)
    down_outmap_single = down_adapter_outmap.astype(jnp.float32)
    lowrank_term_list = jnp.dot(
        hidden_product, down_adapter_inmap, preferred_element_type=jnp.float32
    )
    owned_lowrank_part = lax.psum_scatter(
        lowrank_term_list, "tensor", scatter_dimension=0, tiled=True
    )
    term = jnp.dot(
        hidden_product,
        lax.all_gather(down_projection_matrix, "dp", axis=1, tiled=True),
        preferred_element_type=jnp.float32,
    )
    block_result_rows = lax.psum_scatter(term, "tensor", scatter_dimension=0, tiled=True)
    block_result_rows = block_result_rows + adapter_scale_factor * jnp.dot(
        owned_lowrank_part, down_outmap_single, precision=lax.Precision.HIGHEST
    )
    return block_result_rows.astype(jnp.bfloat16)


def solution(mesh):
    placed = (
        P(("groups", "tensor", "dp"), None),
        P("dp", "tensor"),
        P("dp", "tensor"),
        P("tensor", "dp"),
        P(("groups", "dp"), None),
        P(None, ("groups", "tensor")),
        P(("groups", "dp"), None),
        P(None, ("groups", "tensor")),
        P(("groups", "tensor"), None),
        P(None, "groups"),
    )
    return jax.shard_map(
        body,
        mesh=mesh,
        in_specs=placed,
        out_specs=P(("groups", "tensor", "dp"), None),
        check_vma=False,
    )
```

profile of v0, /device:TPU:0, one launch (start us, length us, event | category | flops | bytes accessed | tf_op | source)
XLA Modules:
  0.0 576.1 jit_solution(376535880790217102)
XLA Ops:
  6.5 4.4 all-to-all-start
  10.9 1.2 copy.13
  12.1 1.2 copy.14
  13.4 44.4 %concatenate.3 = bf16[2048,7296]{1,0:T(8,128)(2,1)} concatenate(bf16[2048,3584]{1,0:T(8,128)(2,1)} %param.11, bf16[2048,3584]{1,0:T(8,128)(2,1)} %param.12, bf16[2048,64]{1,0:T(8,128)(2,1)S(1)} %copy.13, bf16[2048,64]{1,0:T(8,128)(2,1)S(1)} %copy.14), dimensions={1} | concatenate | bytes 59768832 | tf_op jit(solution)/shard_map/concatenate | solution.py:27
  57.8 17.1 %all_gather.6 = bf16[128,2048]{1,0:T(8,128)(2,1)S(1)} all-gather(bf16[32,2048]{1,0:T(8,128)(2,1)S(1)} %bitcast.24), channel_id=1, replica_groups=mesh['groups'=2,'tensor'=4,'dp'=4] {'tensor'}, dimensions={0}, use_global_device_ids=true | all-gather | bytes 655360 | tf_op jit(solution)/shard_map/all_gather | solution.py:31
  74.9 15.4 %fusion.13 = f32[7296,128]{0,1:T(8,128)} fusion(bf16[128,2048]{1,0:T(8,128)(2,1)S(1)} %all_gather.6, bf16[2048,7296]{1,0:T(8,128)(2,1)} %concatenate.3), kind=kOutput, calls=%fused_computation.17 | convolution fusion | flops 3825205248 | bytes 34144256 | tf_op jit(solution)/shard_map/dot_general | solution.py:30
  90.3 0.0 all-reduce.4.cloned.1.call-update
  90.3 0.0 all-gather.2.cloned.1.call-start
  90.4 0.7 all-gather.2.cloned.1.call-update
  91.1 0.0 reduce-scatter.3.cloned.1.call-start
  91.2 0.6 dynamic-slice
  91.7 78.5 %all-reduce.4.cloned.1.call-done = f32[4,4,8,7296]{3,2,1,0:T(8,128)} async-done(((f32[4,4,8,7296]{3,2,1,0:T(8,128)}), f32[4,4,8,7296]{3,2,1,0:T(8,128)}) %all-reduce.4.cloned.1.call-update) | async-done | bytes 3735568
  170.2 1.9 fusion.10
  172.2 0.2 fusion.4
  172.4 0.3 fusion.5
  172.7 0.0 copy-start.4
  172.7 345.2 %all-gather.2.cloned.1.call-done = bf16[3584,8192]{1,0:T(8,128)(2,1)} async-done(((bf16[3584,2048]{1,0:T(8,128)(2,1)}), bf16[3584,8192]{1,0:T(8,128)(2,1)}) %all-gather.2.cloned.1.call-update) | async-done | bytes 58720272 | tf_op jit(solution)/shard_map/all_gather | solution.py:62
  518.0 21.6 %fusion.11 = f32[32,8192]{1,0:T(8,128)} fusion(bf16[32,3584]{1,0:T(8,128)(2,1)S(1)} %fusion.5, bf16[3584,8192]{1,0:T(8,128)(2,1)} %all-gather.2.cloned.1.call-done), kind=kOutput, calls=%fused_computation.15 | convolution fusion | flops 1879048192 | bytes 59998208 | tf_op jit(solution)/shard_map/dot_general | solution.py:60
  539.6 0.0 reduce-scatter.3.cloned.1.call-update
  539.6 0.6 dynamic-slice.2
  540.9 0.2 fusion.12
  541.1 19.7 %all-reduce.1 = f32[32,64]{1,0:T(8,128)S(1)} all-reduce(f32[32,64]{1,0:T(8,128)S(1)} %fusion.12), channel_id=4, replica_groups=mesh['groups'=2,'tensor'=4,'dp'=4] {'tensor'}, use_global_device_ids=true, to_apply=%region_2.3.clone | all-reduce | flops 2048 | bytes 16384
  560.9 6.6 %reduce-scatter.3.cloned.1.call-done = f32[8,8192]{1,0:T(8,128)} async-done(((f32[32,8192]{1,0:T(8,128)}), f32[8,8192]{1,0:T(8,128)}) %reduce-scatter.3.cloned.1.call-update) | async-done | bytes 262160 | tf_op jit(solution)/shard_map/reduce_scatter | solution.py:65
  567.4 2.1 fusion.1
  (13 shorter events, 0.0 us)
Async XLA Ops:
  6.5 560.9 %copy-start = (bf16[64,8192]{1,0:T(8,128)(2,1)S(1)}, bf16[64,8192]{1,0:T(8,128)(2,1)}, u32[]{:S(2)}) copy-start(bf16[64,8192]{1,0:T(8,128)(2,1)} %param.19) | copy-start | bytes 3145732
  6.5 51.2 %all-to-all-start = ((bf16[8,4,2048]{2,0,1:T(8,128)(2,1)}), bf16[8,4,2048]{2,0,1:T(8,128)(2,1)S(1)}, u32[]{:S(2)}, u32[]{:S(2)}) async-start(bf16[8,4,2048]{2,0,1:T(8,128)(2,1)} %bitcast.25), calls=%async_computation | async-start | bytes 262144 | tf_op jit(solution)/shard_map/all_to_all | solution.py:26
  10.9 159.3 %all-reduce.4.cloned.1.call-start = ((), (), s32[]{:S(2)}) async-start(), calls=%async_computation.4 | async-start | bytes 7471104
  57.7 33.4 %copy-start.5 = (u32[32]{0:T(128)S(1)}, u32[32]{0:T(128)}, u32[]{:S(2)}) copy-start(u32[32]{0:T(128)} %constant.9) | copy-start | bytes 388
  57.8 114.4 %copy-start.2 = (bf16[64,3584]{1,0:T(8,128)(2,1)S(1)}, bf16[64,3584]{1,0:T(8,128)(2,1)}, u32[]{:S(2)}) copy-start(bf16[64,3584]{1,0:T(8,128)(2,1)} %param.15) | copy-start | bytes 1376260
  57.8 114.6 %copy-start.3 = (bf16[64,3584]{1,0:T(8,128)(2,1)S(1)}, bf16[64,3584]{1,0:T(8,128)(2,1)}, u32[]{:S(2)}) copy-start(bf16[64,3584]{1,0:T(8,128)(2,1)} %param.17) | copy-start | bytes 1376260
  90.3 427.6 %all-gather.2.cloned.1.call-start = ((), (), s32[]{:S(2)}) async-start(), calls=%async_computation.2 | async-start | bytes 73400320 | tf_op jit(solution)/shard_map/all_gather | solution.py:62
  91.1 476.3 %reduce-scatter.3.cloned.1.call-start = ((), (), s32[]{:S(2)}) async-start(), calls=%async_computation.3 | async-start | bytes 1310720 | tf_op jit(solution)/shard_map/reduce_scatter | solution.py:65
  172.7 366.9 %copy-start.4 = (u32[32]{0:T(128)S(1)}, u32[32]{0:T(128)}, u32[]{:S(2)}) copy-start(u32[32]{0:T(128)} %constant.13) | copy-start | bytes 388
  172.7 368.2 %copy-start.1 = (bf16[3584,64]{0,1:T(8,128)(2,1)S(1)}, bf16[3584,64]{0,1:T(8,128)(2,1)}, u32[]{:S(2)}) copy-start(bf16[3584,64]{0,1:T(8,128)(2,1)} %param.18) | copy-start | bytes 1376260
Sparse Core Ops, SparseCore 0:
  90.5 79.7 all-reduce.3
  171.8 346.1 all-gather.1
  539.8 27.6 reduce-scatter.2
where the time goes:
time: 578 us; the launch traced here: 576 us
  waiting for transfers between devices  431 us (75%)
  local copies, waits for them, and re-layouts  48 us (8%)
  matrix products  39.9 us (7%)
  blocking collectives  36.9 us (6%)
  between operations  13.9 us (2%)
    all_gather x1, waiting for transfers between devices, body(): lax.all_gather(down_projection_matrix, 'dp', axis=1, tiled=True)  345 us
    unnamed x4, waiting for transfers between devices  79.2 us
    concatenate x1, local copies, waits for them, and re-layouts, body(): jnp.concatenate([gate_projection_matrix, up_projection_matrix, gate_adapt...  44.4 us
    dot_general x1, matrix products, body(): jnp.dot(hidden_product, lax.all_gather(down_projection_matrix, 'dp', axis...  21.6 us
    unnamed x1, blocking collectives  19.7 us
    all_gather x1, blocking collectives, body(): lax.all_gather(columns, 'tensor', axis=0, tiled=True)  17.1 us
    dot_general x1, matrix products, body(): jnp.dot(lax.all_gather(columns, 'tensor', axis=0, tiled=True), stacked_lo...  15.4 us
  transfers between devices with their start and end apart: 4, of which 3 were waited for; matrix products, arithmetic and copies ran while one was open for 9% of the time, Pallas kernels for 0%

commit v1 on v0

--- a/solution.py
+++ b/solution.py
@@ -4,6 +4,21 @@
 from jax.sharding import PartitionSpec as P
 
 adapter_scale_factor = 0.5
+
+
+def step_on_weights(obj):
+    mesh_ax = "dp"
+    sides = [obj]
+    axis_len = jax.lax.axis_size(mesh_ax)
+    for s in range(1, axis_len):
+        all_rows = jax.lax.ppermute(
+            sides[s - 1],
+            axis_name=mesh_ax,
+            perm=[(pp, (pp - 1) % axis_len) for pp in range(axis_len)],
+        )
+        sides.append(all_rows)
+    new = jnp.concatenate(sides, axis=1)
+    return jnp.roll(new, jax.lax.axis_index(mesh_ax) * obj.shape[1], axis=1)
 
 
 def body(
@@ -58,9 +73,7 @@
         lowrank_term_list, "tensor", scatter_dimension=0, tiled=True
     )
     term = jnp.dot(
-        hidden_product,
-        lax.all_gather(down_projection_matrix, "dp", axis=1, tiled=True),
-        preferred_element_type=jnp.float32,
+        hidden_product, step_on_weights(down_projection_matrix), preferred_element_type=jnp.float32
     )
     block_result_rows = lax.psum_scatter(term, "tensor", scatter_dimension=0, tiled=True)
     block_result_rows = block_result_rows + adapter_scale_factor * jnp.dot(

time: 578 us -> 764 us (1.32)
  local copies, waits for them, and re-layouts: 48 us -> 161 us
  waiting for transfers between devices: 431 us -> 500 us
    all_gather x1 -> x0, waiting for transfers between devices: 345 us -> none  [body(): lax.all_gather(down_projection_matrix, 'dp', axis=1, tiled=True)]
    ppermute x0 -> x3, waiting for transfers between devices: none -> 317 us  [step_on_weights(): jax.lax.ppermute(sides[s - 1], axis_name=mesh_ax, perm=[(pp, (pp - 1) % a...]
    all_to_all x1, waiting for transfers between devices: 0.01 us -> 111 us  [body(): lax.all_to_all(tokens, 'dp', split_axis=1, concat_axis=0, tiled=True)]
    unnamed x16 -> x23, local copies, waits for them, and re-layouts: 3.65 us -> 104 us
    unnamed x4 -> x3, waiting for transfers between devices: 79.2 us -> 65.1 us
    concatenate x0 -> x1, local copies, waits for them, and re-layouts: none -> 13.4 us  [step_on_weights(): return jnp.roll(new, jax.lax.axis_index(mesh_ax) * obj.shape[1], axis=1)]
  transfers between devices with their start and end apart: 4 -> 6, of which waited for: 3 -> 5; matrix products, arithmetic and copies ran while one was open for 9% -> 14% of each run, Pallas kernels for 0% -> 0%
where the time goes in v1:
time: 764 us; the launch traced here: 762 us
  waiting for transfers between devices  500 us (65%)
  local copies, waits for them, and re-layouts  161 us (21%)
  matrix products  38.4 us (5%)
  blocking collectives  34.9 us (5%)
  between operations  14.2 us (2%)
  starting transfers between devices  9.62 us (1%)
    ppermute x3, waiting for transfers between devices, step_on_weights(): jax.lax.ppermute(sides[s - 1], axis_name=mesh_ax, perm=[(pp, (pp - 1) % a...  317 us
    all_to_all x1, waiting for transfers between devices, body(): lax.all_to_all(tokens, 'dp', split_axis=1, concat_axis=0, tiled=True)  111 us
    unnamed x23, local copies, waits for them, and re-layouts  104 us
    unnamed x3, waiting for transfers between devices  65.1 us
    concatenate x1, local copies, waits for them, and re-layouts, body(): jnp.concatenate([gate_projection_matrix, up_projection_matrix, gate_adapt...  44.4 us
    dot_general x1, matrix products, body(): jnp.dot(hidden_product, step_on_weights(down_projection_matrix), preferre...  21.7 us
    unnamed x1, blocking collectives  19.3 us
    all_gather x1, blocking collectives, body(): lax.all_gather(columns, 'tensor', axis=0, tiled=True)  15.6 us
  transfers between devices with their start and end apart: 6, of which 5 were waited for; matrix products, arithmetic and copies ran while one was open for 14% of the time, Pallas kernels for 0%

profile of v1, /device:TPU:0, one launch (start us, length us, event | category | flops | bytes accessed | tf_op | source)
XLA Modules:
  0.0 762.0 jit_solution(3875969877405818917)
XLA Ops:
  6.5 2.4 collective-permute-start
  8.9 158.7 %collective-permute-done = bf16[3584,2048]{1,0:T(8,128)(2,1)S(1)} collective-permute-done((bf16[3584,2048]{1,0:T(8,128)(2,1)}, bf16[3584,2048]{1,0:T(8,128)(2,1)S(1)}, u32[]{:S(2)}, u32[]{:S(2)}) %collective-permute-start) | collective-permute-done | bytes 14680096 | tf_op jit(solution)/shard_map/ppermute | solution.py:14
  167.6 5.2 copy-done.1
  172.9 1.8 collective-permute-start.1
  174.7 158.4 %collective-permute-done.1 = bf16[3584,2048]{1,0:T(8,128)(2,1)} collective-permute-done((bf16[3584,2048]{1,0:T(8,128)(2,1)S(1)}, bf16[3584,2048]{1,0:T(8,128)(2,1)}, u32[]{:S(2)}, u32[]{:S(2)}) %collective-permute-start.1) | collective-permute-done | bytes 14680096 | tf_op jit(solution)/shard_map/ppermute | solution.py:14
  333.0 2.0 collective-permute-start.2
  335.1 3.3 all-to-all-start
  340.9 44.4 %concatenate.9 = bf16[2048,7296]{1,0:T(8,128)(2,1)} concatenate(bf16[2048,3584]{1,0:T(8,128)(2,1)} %param.11, bf16[2048,3584]{1,0:T(8,128)(2,1)} %param.12, bf16[2048,64]{1,0:T(8,128)(2,1)S(1)} %copy.13, bf16[2048,64]{1,0:T(8,128)(2,1)S(1)} %copy.14), dimensions={1} | concatenate | bytes 59768832 | tf_op jit(solution)/shard_map/concatenate | solution.py:42
  385.3 110.8 %all-to-all-done = bf16[8,4,2048]{2,0,1:T(8,128)(2,1)S(1)} async-done(((bf16[8,4,2048]{2,0,1:T(8,128)(2,1)}), bf16[8,4,2048]{2,0,1:T(8,128)(2,1)S(1)}, u32[]{:S(2)}, u32[]{:S(2)}) %all-to-all-start) | async-done | bytes 131104 | tf_op jit(solution)/shard_map/all_to_all | solution.py:41
  496.1 15.6 %all_gather.3 = bf16[128,2048]{1,0:T(8,128)(2,1)S(1)} all-gather(bf16[32,2048]{1,0:T(8,128)(2,1)S(1)} %bitcast.23), channel_id=1, replica_groups=mesh['groups'=2,'tensor'=4,'dp'=4] {'tensor'}, dimensions={0}, use_global_device_ids=true | all-gather | bytes 655360 | tf_op jit(solution)/shard_map/all_gather | solution.py:46
  511.7 15.5 %fusion.13 = f32[7296,128]{0,1:T(8,128)} fusion(bf16[128,2048]{1,0:T(8,128)(2,1)S(1)} %all_gather.3, bf16[2048,7296]{1,0:T(8,128)(2,1)} %concatenate.9), kind=kOutput, calls=%fused_computation.26 | convolution fusion | flops 3825205248 | bytes 34144256 | tf_op jit(solution)/shard_map/dot_general | solution.py:45
  528.6 13.5 %constant_dynamic-update-slice_fusion.7 = bf16[3584,16384]{1,0:T(8,128)(2,1)} fusion(bf16[3584,2048]{1,0:T(8,128)(2,1)} %param.13), kind=kLoop, calls=%fused_computation.18 | loop fusion | bytes 29360128
  542.1 65.1 %all-reduce.4.cloned.1.call-done = f32[4,4,8,7296]{3,2,1,0:T(8,128)} async-done(((f32[4,4,8,7296]{3,2,1,0:T(8,128)}), f32[4,4,8,7296]{3,2,1,0:T(8,128)}) %all-reduce.4.cloned.1.call-update) | async-done | bytes 3735568
  607.2 1.9 fusion.11
  609.7 13.4 %constant_dynamic-update-slice_fusion.6 = bf16[3584,16384]{1,0:T(8,128)(2,1)} fusion(bf16[3584,16384]{1,0:T(8,128)(2,1)} %constant_dynamic-update-slice_fusion.7, bf16[3584,2048]{1,0:T(8,128)(2,1)} %copy-done.1), kind=kLoop, calls=%fused_computation.17 | loop fusion | bytes 29360128
  623.1 13.5 %constant_dynamic-update-slice_fusion.5 = bf16[3584,16384]{1,0:T(8,128)(2,1)} fusion(bf16[3584,16384]{1,0:T(8,128)(2,1)} %constant_dynamic-update-slice_fusion.6, bf16[3584,2048]{1,0:T(8,128)(2,1)} %collective-permute-done.1), kind=kLoop, calls=%fused_computation.16 | loop fusion | bytes 29360128
  636.6 13.4 %constant_dynamic-update-slice_fusion.4 = bf16[3584,16384]{1,0:T(8,128)(2,1)} fusion(bf16[3584,16384]{1,0:T(8,128)(2,1)} %constant_dynamic-update-slice_fusion.5, bf16[3584,2048]{1,0:T(8,128)(2,1)} %collective-permute-done.2), kind=kLoop, calls=%fused_computation.15 | loop fusion | bytes 29360128
  650.0 13.4 %constant_dynamic-update-slice_fusion.3 = bf16[3584,16384]{1,0:T(8,128)(2,1)} fusion(bf16[3584,16384]{1,0:T(8,128)(2,1)} %constant_dynamic-update-slice_fusion.4, bf16[3584,2048]{1,0:T(8,128)(2,1)} %param.13), kind=kLoop, calls=%fused_computation.14 | loop fusion | bytes 29360128
  663.4 13.4 %constant_dynamic-update-slice_fusion.2 = bf16[3584,16384]{1,0:T(8,128)(2,1)} fusion(bf16[3584,16384]{1,0:T(8,128)(2,1)} %constant_dynamic-update-slice_fusion.3, bf16[3584,2048]{1,0:T(8,128)(2,1)} %copy-done.1), kind=kLoop, calls=%fused_computation.13 | loop fusion | bytes 29360128
  676.8 13.4 %constant_dynamic-update-slice_fusion.1 = bf16[3584,16384]{1,0:T(8,128)(2,1)} fusion(bf16[3584,16384]{1,0:T(8,128)(2,1)} %constant_dynamic-update-slice_fusion.2, bf16[3584,2048]{1,0:T(8,128)(2,1)} %collective-permute-done.1), kind=kLoop, calls=%fused_computation.12 | loop fusion | bytes 29360128
  690.2 13.4 %constant_dynamic-update-slice_fusion = bf16[3584,16384]{1,0:T(8,128)(2,1)} fusion(bf16[3584,16384]{1,0:T(8,128)(2,1)} %constant_dynamic-update-slice_fusion.1, bf16[3584,2048]{1,0:T(8,128)(2,1)} %collective-permute-done.2), kind=kLoop, calls=%fused_computation.11 | loop fusion | bytes 29360128 | tf_op jit(solution)/shard_map/jit(_roll_dynamic)/concatenate | solution.py:21
  703.7 21.7 %fusion = f32[32,8192]{1,0:T(8,128)} fusion(bf16[32,3584]{1,0:T(8,128)(2,1)S(1)} %fusion.5, bf16[3584,16384]{1,0:T(8,128)(2,1)} %constant_dynamic-update-slice_fusion, s32[]{:T(128)S(6)} %select_n.14), kind=kOutput, calls=%fused_computation | convolution fusion | flops 1879048192 | bytes 59998212 | tf_op jit(solution)/shard_map/dot_general | solution.py:75
  726.8 19.3 %all-reduce.1 = f32[32,64]{1,0:T(8,128)S(1)} all-reduce(f32[32,64]{1,0:T(8,128)S(1)} %fusion.12), channel_id=4, replica_groups=mesh['groups'=2,'tensor'=4,'dp'=4] {'tensor'}, use_global_device_ids=true, to_apply=%region_2.3.clone | all-reduce | flops 2048 | bytes 16384
  746.7 6.8 reduce-scatter.3.cloned.1.call-done
  (25 shorter events, 7.3 us)
Async XLA Ops:
  6.5 739.6 %copy-start = (bf16[64,8192]{1,0:T(8,128)(2,1)S(1)}, bf16[64,8192]{1,0:T(8,128)(2,1)}, u32[]{:S(2)}) copy-start(bf16[64,8192]{1,0:T(8,128)(2,1)} %param.19) | copy-start | bytes 3145732
  6.5 602.6 %copy-start.3 = (bf16[64,3584]{1,0:T(8,128)(2,1)S(1)}, bf16[64,3584]{1,0:T(8,128)(2,1)}, u32[]{:S(2)}) copy-start(bf16[64,3584]{1,0:T(8,128)(2,1)} %param.15) | copy-start | bytes 1376260
  6.5 602.8 %copy-start.4 = (bf16[64,3584]{1,0:T(8,128)(2,1)S(1)}, bf16[64,3584]{1,0:T(8,128)(2,1)}, u32[]{:S(2)}) copy-start(bf16[64,3584]{1,0:T(8,128)(2,1)} %param.17) | copy-start | bytes 1376260
  6.5 161.1 %collective-permute-start = (bf16[3584,2048]{1,0:T(8,128)(2,1)}, bf16[3584,2048]{1,0:T(8,128)(2,1)S(1)}, u32[]{:S(2)}, u32[]{:S(2)}) collective-permute-start(bf16[3584,2048]{1,0:T(8,128)(2,1)} %param.13), channel_id=1, source_target_pairs={{0,3},{1,0},{2,1},{3,2},{4,7},{5,4},{6,5},{7,6},{8,11},{9,8},{10,9... | collective-permute-start | bytes 44040200 | tf_op jit(solution)/shard_map/ppermute | solution.py:14
  167.6 5.2 copy-start.1
  172.9 160.2 %collective-permute-start.1 = (bf16[3584,2048]{1,0:T(8,128)(2,1)S(1)}, bf16[3584,2048]{1,0:T(8,128)(2,1)}, u32[]{:S(2)}, u32[]{:S(2)}) collective-permute-start(bf16[3584,2048]{1,0:T(8,128)(2,1)S(1)} %collective-permute-done), channel_id=1, source_target_pairs={{0,3},{1,0},{2,1},{3,2},{4,7},{5,4},{6,5},{7,6},{8,11},{9,8},{10,9... | collective-permute-start | bytes 44040200 | tf_op jit(solution)/shard_map/ppermute | solution.py:14
  333.0 303.5 %collective-permute-start.2 = (bf16[3584,2048]{1,0:T(8,128)(2,1)}, bf16[3584,2048]{1,0:T(8,128)(2,1)}, u32[]{:S(2)}, u32[]{:S(2)}) collective-permute-start(bf16[3584,2048]{1,0:T(8,128)(2,1)} %collective-permute-done.1), channel_id=1, source_target_pairs={{0,3},{1,0},{2,1},{3,2},{4,7},{5,4},{6,5},{7,6},{8,11},{9,8},{10,9... | collective-permute-start | bytes 44040200 | tf_op jit(solution)/shard_map/ppermute | solution.py:14
  335.1 161.0 %all-to-all-start = ((bf16[8,4,2048]{2,0,1:T(8,128)(2,1)}), bf16[8,4,2048]{2,0,1:T(8,128)(2,1)S(1)}, u32[]{:S(2)}, u32[]{:S(2)}) async-start(bf16[8,4,2048]{2,0,1:T(8,128)(2,1)} %bitcast.24), calls=%async_computation | async-start | bytes 262144 | tf_op jit(solution)/shard_map/all_to_all | solution.py:41
  338.4 268.8 %all-reduce.4.cloned.1.call-start = ((), (), s32[]{:S(2)}) async-start(), calls=%async_computation.3 | async-start | bytes 7471104
  527.3 226.2 %reduce-scatter.3.cloned.1.call-start = ((), (), s32[]{:S(2)}) async-start(), calls=%async_computation.2 | async-start | bytes 1310720 | tf_op jit(solution)/shard_map/reduce_scatter | solution.py:78
  623.1 102.3 %copy-start.5 = (u32[32]{0:T(128)S(1)}, u32[32]{0:T(128)}, u32[]{:S(2)}) copy-start(u32[32]{0:T(128)} %constant.41) | copy-start | bytes 388
  623.1 103.5 %copy-start.2 = (bf16[3584,64]{0,1:T(8,128)(2,1)S(1)}, bf16[3584,64]{0,1:T(8,128)(2,1)}, u32[]{:S(2)}) copy-start(bf16[3584,64]{0,1:T(8,128)(2,1)} %param.18) | copy-start | bytes 1376260
Sparse Core Ops, SparseCore 0:
  527.4 79.7 all-reduce.3
  725.5 27.9 reduce-scatter.2
